TPU v7x, 32 devices: a whole 2x2x4 slice. The times are simulated.
32 devices in a mesh: ctx: 8 (over y, x, core), chan: 4 (over z).
Axes of the slice: x: 2, y: 2, z: 4, core: 2. Of those that a mesh axis runs over, the one named last changes fastest.
Arguments:
- signal: float32 [2048, 2048], P('chan', 'ctx'), may hold values from -6 to 6
- gate_in: float32 [2048, 2048], P('chan', 'ctx'), may hold values from -6 to 6
- filter_raw: float32 [2048, 2048], P('chan', 'ctx'), may hold values from -6 to 6
- short_kernel: float32 [2048, 7], P('chan'), may hold values from -2 to 2
- skip_gain: float32 [2048], P('chan'), may hold values from -4 to 4
- out_weight: float32 [2048, 2048], P(None, 'chan'), may hold values from -0.125 to 0.125
- cotangent: float32 [2048, 2048], P('chan', 'ctx'), may hold values from -6 to 6
Outputs:
- grad_gate: float32 [2048, 2048], P('chan', 'ctx')
- grad_signal: float32 [2048, 2048], P('chan', 'ctx')
- grad_filter: float32 [2048, 2048], P('chan', 'ctx')
- grad_kernel: float32 [2048, 7], P('chan')
- grad_skip: float32 [2048], P('chan')
All inputs are finite; a program needn't handle non-finite values.
Results may differ from a plain program's by a relative error of at most 0.00011.
Values sent between devices are 32-bit elements; how exact they have to be, the bound alone decides.
A program may use at most 128 MiB of HBM per device.

v0:
```python
import math
import jax
import jax.numpy as jnp
from jax import lax
from jax.sharding import PartitionSpec as P

HIGH = lax.Precision.HIGHEST


def passed_along(block, axis, distance):
    devices = range(lax.axis_size(axis))
    route = [(i - distance, i) for i in devices if i - distance in devices]
    return lax.ppermute(block, axis, route)


def angle_table(rows_len, cols_len, modulus):
    products = (
        jnp.arange(rows_len, dtype=jnp.int32)[:, None]
        * jnp.arange(cols_len, dtype=jnp.int32)[None, :]
        % modulus
    )
    return 2.0 * math.pi / modulus * products.astype(jnp.float32)


def rotate(real_part, imag_part, angles, sign):
    cosine = jnp.cos(angles)
    sine = sign * jnp.sin(angles)
    return (real_part * cosine - imag_part * sine, real_part * sine + imag_part * cosine)


def mix_last(real_part, imag_part, sign):
    span_len = real_part.shape[-1]
    angles = angle_table(span_len, span_len, span_len)
    cosine = jnp.cos(angles)
    sine = sign * jnp.sin(angles)

    def product_with(operand, table):
        return jnp.einsum("...a,ab->...b", operand, table, precision=HIGH)

    return (
        product_with(real_part, cosine) - product_with(imag_part, sine),
        product_with(real_part, sine) + product_with(imag_part, cosine),
    )


def mix_middle(real_part, imag_part, sign):
    span_len = real_part.shape[-2]
    angles = angle_table(span_len, span_len, span_len)
    cosine = jnp.cos(angles)
    sine = sign * jnp.sin(angles)

    def product_with(operand, table):
        return jnp.einsum("...ac,ab->...bc", operand, table, precision=HIGH)

    return (
        product_with(real_part, cosine) - product_with(imag_part, sine),
        product_with(real_part, sine) + product_with(imag_part, cosine),
    )


def split_len(length):
    inner_len = 128
    return (length // inner_len, inner_len)


def local_forward(real_part, imag_part):
    leading = real_part.shape[:-1]
    length = real_part.shape[-1]
    outer_len, inner_len = split_len(length)
    real_part = real_part.reshape(leading + (outer_len, inner_len))
    imag_part = imag_part.reshape(leading + (outer_len, inner_len))
    real_part, imag_part = mix_middle(real_part, imag_part, -1.0)
    real_part, imag_part = rotate(
        real_part, imag_part, angle_table(outer_len, inner_len, length), -1.0
    )
    real_part, imag_part = mix_last(real_part, imag_part, -1.0)
    return (real_part.reshape(leading + (length,)), imag_part.reshape(leading + (length,)))


def local_inverse(real_part, imag_part):
    leading = real_part.shape[:-1]
    length = real_part.shape[-1]
    outer_len, inner_len = split_len(length)
    real_part = real_part.reshape(leading + (outer_len, inner_len))
    imag_part = imag_part.reshape(leading + (outer_len, inner_len))
    real_part, imag_part = mix_last(real_part, imag_part, 1.0)
    real_part, imag_part = rotate(
        real_part, imag_part, angle_table(outer_len, inner_len, length), 1.0
    )
    real_part, imag_part = mix_middle(real_part, imag_part, 1.0)
    return (real_part.reshape(leading + (length,)), imag_part.reshape(leading + (length,)))


def block_twiddle(freqs, slice_len, modulus):
    offsets = lax.axis_index("ctx") * slice_len + jnp.arange(slice_len, dtype=jnp.int32)
    products = jnp.arange(freqs, dtype=jnp.int32)[:, None] * offsets[None, :] % modulus
    return 2.0 * math.pi / modulus * products.astype(jnp.float32)


def spectra(stacked):
    n_arrays, channels, length = stacked.shape
    devices = lax.axis_size("ctx")
    slice_len = length // devices
    freqs = 2 * devices
    modulus = freqs * length
    pieces = jnp.transpose(stacked.reshape(n_arrays, channels, devices, slice_len), (0, 2, 3, 1))
    arrived = lax.all_to_all(pieces, "ctx", split_axis=1, concat_axis=1, tiled=True)
    angles = angle_table(freqs, devices, freqs)
    real_part = jnp.einsum("qp,kprc->kqrc", jnp.cos(angles), arrived, precision=HIGH)
    imag_part = -jnp.einsum("qp,kprc->kqrc", jnp.sin(angles), arrived, precision=HIGH)
    twiddle = block_twiddle(freqs, slice_len, modulus)[:, :, None]
    real_part, imag_part = rotate(real_part, imag_part, twiddle, -1.0)
    arrived = lax.all_to_all(
        jnp.stack((real_part, imag_part)), "ctx", split_axis=2, concat_axis=3, tiled=True
    )
    arrived = jnp.moveaxis(arrived, 4, 2)
    return local_forward(arrived[0], arrived[1])


def signals(real_part, imag_part):
    real_part, imag_part = local_inverse(real_part, imag_part)
    n_arrays, channels, local_freqs, length = real_part.shape
    devices = lax.axis_size("ctx")
    slice_len = length // devices
    freqs = 2 * devices
    modulus = freqs * length
    stacked = jnp.moveaxis(jnp.stack((real_part, imag_part)), 2, 4)
    arrived = lax.all_to_all(stacked, "ctx", split_axis=3, concat_axis=2, tiled=True)
    twiddle = block_twiddle(freqs, slice_len, modulus)[:, :, None]
    real_part, imag_part = rotate(arrived[0], arrived[1], twiddle, 1.0)
    angles = angle_table(devices, freqs, freqs)
    samples = jnp.einsum("pq,kqrc->kprc", jnp.cos(angles), real_part, precision=HIGH) - jnp.einsum(
        "pq,kqrc->kprc", jnp.sin(angles), imag_part, precision=HIGH
    )
    arrived = lax.all_to_all(samples, "ctx", split_axis=1, concat_axis=2, tiled=True)
    return jnp.transpose(arrived.reshape(n_arrays, length, channels), (0, 2, 1)) / modulus


def spec_product(first, second, conjugate):
    first_real, first_imag = first
    if conjugate:
        first_imag = -first_imag
    second_real, second_imag = second
    return (
        first_real * second_real - first_imag * second_imag,
        first_real * second_imag + first_imag * second_real,
    )


def per_device(signal, gate_in, filter_raw, short_kernel, skip_gain, out_weight, cotangent):
    channels, length = signal.shape
    kernel_taps = short_kernel.shape[1]
    scale_factor = 1.0 / math.sqrt(length * lax.axis_size("ctx"))
    left_rim = passed_along(signal[:, length - (kernel_taps - 1) :], "ctx", 1)
    padded = jnp.concatenate((left_rim, signal), axis=1)
    conv_in = jnp.zeros_like(signal)
    for j in range(kernel_taps):
        conv_in = (
            conv_in
            + short_kernel[:, j : j + 1]
            * padded[:, kernel_taps - 1 - j : kernel_taps - 1 - j + length]
        )
    long_filter = filter_raw * scale_factor
    spec_real, spec_imag = spectra(jnp.stack((long_filter, conv_in)))
    filter_spec = (spec_real[0], spec_imag[0])
    value_spec = (spec_real[1], spec_imag[1])
    conv_real, conv_imag = spec_product(filter_spec, value_spec, False)
    long_conv = signals(conv_real[None], conv_imag[None])[0]
    grad_mix = jnp.dot(
        out_weight.T,
        lax.all_gather(cotangent, "chan", axis=0, tiled=True),
        precision=HIGH,
        preferred_element_type=jnp.float32,
    )
    grad_resp = grad_mix * gate_in
    grad_real, grad_imag = spectra(grad_resp[None])
    grad_spec = (grad_real[0], grad_imag[0])
    corr_spec = spec_product(filter_spec, grad_spec, True)
    filt_grad_spec = spec_product(value_spec, grad_spec, True)
    outputs = signals(
        jnp.stack((corr_spec[0], filt_grad_spec[0])), jnp.stack((corr_spec[1], filt_grad_spec[1]))
    )
    corr_part = outputs[0]
    filter_part = outputs[1]
    response = long_conv + skip_gain[:, None] * conv_in
    grad_gate = grad_mix * response
    grad_value = corr_part + skip_gain[:, None] * grad_resp
    grad_filter = filter_part * scale_factor
    right_rim = passed_along(grad_value[:, : kernel_taps - 1], "ctx", -1)
    extended = jnp.concatenate((grad_value, right_rim), axis=1)
    grad_signal = jnp.zeros_like(grad_value)
    for j in range(kernel_taps):
        grad_signal = grad_signal + short_kernel[:, j : j + 1] * extended[:, j : j + length]
    kernel_part = jnp.stack(
        [
            jnp.sum(
                grad_value * padded[:, kernel_taps - 1 - j : kernel_taps - 1 - j + length], axis=1
            )
            for j in range(kernel_taps)
        ],
        axis=1,
    )
    skip_part = jnp.sum(grad_resp * conv_in, axis=1)
    skip_sum, kernel_sum = lax.psum((skip_part, kernel_part), "ctx")
    return (grad_gate, grad_signal, grad_filter, kernel_sum * scale_factor, skip_sum * scale_factor)


def solution(mesh):
    placed = (
        P("chan", "ctx"),
        P("chan", "ctx"),
        P("chan", "ctx"),
        P("chan", None),
        P("chan"),
        P(None, "chan"),
        P("chan", "ctx"),
    )
    return jax.shard_map(
        per_device,
        mesh=mesh,
        in_specs=placed,
        out_specs=(
            P("chan", "ctx"),
            P("chan", "ctx"),
            P("chan", "ctx"),
            P("chan", None),
            P("chan"),
        ),
        check_vma=False,
    )
```

profile of v0, /device:TPU:1, one launch (start us, length us, event | category | flops | bytes accessed | tf_op | source)
XLA Modules:
  0.0 497.2 jit_solution(16550516221013616435)
XLA Ops:
  16.0 41.6 %all-gather.2.cloned.1.call-done = f32[2048,256]{1,0:T(8,128)} async-done(((f32[512,256]{1,0:T(8,128)}), f32[2048,256]{1,0:T(8,128)}) %all-gather.2.cloned.1.call-update) | async-done | bytes 2097168 | tf_op jit(solution)/shard_map/all_gather | solution.py:171
  57.6 8.1 %multiply_reduce_fusion = (f32[512]{0:T(512)S(1)}, f32[512,256]{0,1:T(8,128)}, f32[512,256]{0,1:T(8,128)S(1)}, f32[512,256]{0,1:T(8,128)}) fusion(f32[512,256]{0,1:T(8,128)S(1)} %copy.214, f32[512,256]{0,1:T(8,128)S(1)} %copy.185, f32[512,6]{0,1:T(8,128)S(1)} %collective-permute-done, f32[512]{0:T(512)S(1)} %bitcast.367, f32[512]{0:T(512)S(1)} %bitcast.369, ...), kind=kOutput, calls=%fused_computation.166 | convolution fusion | flops 3224108544 | bytes 8941568 | tf_op jit(solution)/shard_map/dot_general | solution.py:169
  76.7 6.5 %all-to-all-start = ((f32[2,8,32,512]{3,2,0,1:T(8,128)}), f32[2,8,32,512]{3,2,0,1:T(8,128)S(1)}, u32[]{:S(2)}, u32[]{:S(2)}) async-start(f32[2,8,32,512]{3,2,0,1:T(8,128)} %copy.188), calls=%async_computation | async-start | bytes 2097152 | tf_op jit(solution)/shard_map/all_to_all | solution.py:107
  95.1 7.3 %all-to-all-start.5 = ((f32[2,1,16,32,512]{4,3,1,0,2:T(8,128)}), f32[2,1,16,32,512]{4,3,1,0,2:T(8,128)S(1)}, u32[]{:S(2)}, u32[]{:S(2)}) async-start(f32[2,1,16,32,512]{4,3,1,0,2:T(8,128)} %copy.217), calls=%async_computation.5 | async-start | bytes 4194304 | tf_op jit(solution)/shard_map/all_to_all | solution.py:113
  113.0 12.5 %all-to-all-done.5 = f32[2,1,16,32,512]{4,3,1,0,2:T(8,128)S(1)} async-done(((f32[2,1,16,32,512]{4,3,1,0,2:T(8,128)}), f32[2,1,16,32,512]{4,3,1,0,2:T(8,128)S(1)}, u32[]{:S(2)}, u32[]{:S(2)}) %all-to-all-start.5) | async-done | bytes 2097184 | tf_op jit(solution)/shard_map/all_to_all | solution.py:113
  125.5 8.3 %all-to-all-start.1 = ((f32[2,2,16,32,512]{4,3,1,0,2:T(8,128)}), f32[2,2,16,32,512]{4,3,1,0,2:T(8,128)}, u32[]{:S(2)}, u32[]{:S(2)}) async-start(f32[2,2,16,32,512]{4,3,1,0,2:T(8,128)} %copy.191), calls=%async_computation.1 | async-start | bytes 8388608 | tf_op jit(solution)/shard_map/all_to_all | solution.py:113
  148.0 6.0 %add_bitcast_fusion.2 = (f32[512,2,2,128]{3,2,1,0:T(2,128)S(1)}, f32[512,2,2,128]{3,2,1,0:T(2,128)S(1)}) fusion(f32[2,1,512,2,128]{4,0,3,2,1:T(2,128)S(1)} %fusion.48, f32[2,128]{1,0:T(2,128)S(1)} %get-tuple-element.83, f32[2,128]{1,0:T(2,128)S(1)} %get-tuple-element.84, f32[2,512,2,128]{3,0,2,1:T(2,128)S(1)} %fusion.208, f32[512,2,2,128]{3,2,1,0:T(2,128)} %copy-done.15), kind=kOutput, calls=%fused_computation.105 | convolution fusion | flops 8126520 | bytes 5244928 | tf_op jit(solution)/shard_map/...ac,ab->...bc/dot_general | solution.py:53
  159.8 19.6 %all-to-all-done.1 = f32[2,2,16,32,512]{4,3,1,0,2:T(8,128)} async-done(((f32[2,2,16,32,512]{4,3,1,0,2:T(8,128)}), f32[2,2,16,32,512]{4,3,1,0,2:T(8,128)}, u32[]{:S(2)}, u32[]{:S(2)}) %all-to-all-start.1) | async-done | bytes 4194336 | tf_op jit(solution)/shard_map/all_to_all | solution.py:113
  187.9 8.8 %fusion.221 = f32[2,2,512,2,128]{4,0,3,2,1:T(2,128)} fusion(f32[2,512,2,2,128]{4,3,2,1,0:T(2,128)S(1)} %copy.258), kind=kOutput, calls=%fused_computation.285 | convolution fusion | flops 12582968 | bytes 4194304 | tf_op jit(solution)/shard_map/...ac,ab->...bc/dot_general | solution.py:53
  196.7 8.7 %fusion.223 = f32[2,2,512,2,128]{4,0,3,2,1:T(2,128)} fusion(f32[2,512,2,2,128]{4,3,2,1,0:T(2,128)S(1)} %copy.258), kind=kOutput, calls=%fused_computation.287 | convolution fusion | flops 12582972 | bytes 4194304 | tf_op jit(solution)/shard_map/...ac,ab->...bc/dot_general | solution.py:53
  208.5 9.6 %convolution_subtract_fusion = f32[2,2,512,2,128]{4,0,3,2,1:T(2,128)S(1)} fusion(f32[2,2,512,2,128]{4,0,3,2,1:T(2,128)} %fusion.221, f32[2,512,2,2,128]{4,3,2,1,0:T(2,128)S(1)} %copy.259), kind=kOutput, calls=%fused_computation.43 | convolution fusion | flops 13107260 | bytes 6291456 | tf_op jit(solution)/shard_map/...ac,ab->...bc/dot_general | solution.py:53
  218.1 9.9 %subtract_bitcast_fusion.1 = (f32[2,512,2,2,128]{4,3,2,1,0:T(2,128)S(1)}, f32[2,512,2,2,128]{4,3,2,1,0:T(2,128)S(1)}) fusion(f32[2,2,512,2,128]{4,0,3,2,1:T(2,128)S(1)} %convolution_subtract_fusion, f32[2,128]{1,0:T(2,128)S(1)} %get-tuple-element.83, f32[2,128]{1,0:T(2,128)S(1)} %get-tuple-element.84, f32[2,2,512,2,128]{4,0,3,2,1:T(2,128)S(1)} %copy-done.12, ...), kind=kOutput, calls=%fused_computation.27 | convolution fusion | flops 16252984 | bytes 10487808 | tf_op jit(solution)/shard_map/...ac,ab->...bc/dot_general | solution.py:53
  269.8 7.0 %fusion.49 = f32[1,512,2,2,128]{4,3,2,1,0:T(2,128)} fusion(f32[2,512,2,128]{3,0,2,1:T(2,128)} %fusion.79, f32[512,2,2,128]{3,0,2,1:T(8,128)} %copy-done.14), kind=kOutput, calls=%fused_computation.78 | convolution fusion | flops 6553656 | bytes 3145728 | tf_op jit(solution)/shard_map/...ac,ab->...bc/dot_general | solution.py:53
  284.3 7.9 %all-to-all-start.2 = ((f32[2,1,2,256,512]{4,2,0,1,3:T(2,128)}), f32[2,1,2,256,512]{4,2,0,1,3:T(2,128)}, u32[]{:S(2)}, u32[]{:S(2)}) async-start(f32[2,1,2,256,512]{4,2,0,1,3:T(2,128)} %maximum_bitcast_fusion.1), calls=%async_computation.2 | async-start | bytes 4194304 | tf_op jit(solution)/shard_map/all_to_all | solution.py:128
  299.7 8.1 %fusion.36 = f32[2,2,512,2,128]{4,0,3,2,1:T(2,128)S(1)} fusion(f32[2,512,2,2,128]{4,1,3,2,0:T(8,128)S(1)} %get-tuple-element.50), kind=kOutput, calls=%fused_computation.50 | convolution fusion | flops 12582968 | bytes 4194304 | tf_op jit(solution)/shard_map/...ac,ab->...bc/dot_general | solution.py:53
  307.8 9.8 %subtract_bitcast_fusion = f32[2,512,2,2,128]{4,3,2,1,0:T(2,128)} fusion(f32[2,2,512,2,128]{4,0,3,2,1:T(2,128)S(1)} %fusion.36, f32[2,512,2,2,128]{4,1,3,2,0:T(8,128)S(1)} %get-tuple-element.49), kind=kOutput, calls=%fused_computation.23 | convolution fusion | flops 13107256 | bytes 6291456 | tf_op jit(solution)/shard_map/...ac,ab->...bc/dot_general | solution.py:53
  317.6 6.1 %copy.264 = f32[2,512,2,2,128]{1,2,0,4,3:T(2,128)} copy(f32[2,512,2,2,128]{4,3,2,1,0:T(2,128)} %subtract_bitcast_fusion) | data formatting | bytes 4194304 | tf_op jit(solution)/shard_map/stack;reshape | solution.py:127
  323.7 8.0 %fusion.34 = f32[2,2,512,2,128]{4,0,3,2,1:T(2,128)S(1)} fusion(f32[2,512,2,2,128]{4,1,3,2,0:T(8,128)S(1)} %get-tuple-element.50), kind=kOutput, calls=%fused_computation.48 | convolution fusion | flops 12582968 | bytes 4194304 | tf_op jit(solution)/shard_map/...ac,ab->...bc/dot_general | solution.py:53
  331.8 9.9 %add_bitcast_fusion = f32[2,512,2,2,128]{4,3,2,1,0:T(2,128)} fusion(f32[2,2,512,2,128]{4,0,3,2,1:T(2,128)S(1)} %fusion.34, f32[2,512,2,2,128]{4,1,3,2,0:T(8,128)S(1)} %copy-done.11), kind=kOutput, calls=%fused_computation.22 | convolution fusion | flops 13107256 | bytes 6291456 | tf_op jit(solution)/shard_map/...ac,ab->...bc/dot_general | solution.py:53
  341.7 6.3 %copy.265 = f32[2,512,2,2,128]{1,2,0,4,3:T(2,128)} copy(f32[2,512,2,2,128]{4,3,2,1,0:T(2,128)} %add_bitcast_fusion) | data formatting | bytes 4194304 | tf_op jit(solution)/shard_map/stack;reshape | solution.py:127
  365.2 38.7 %all-to-all-done.6 = f32[2,2,2,256,512]{4,2,1,0,3:T(2,128)} async-done(((f32[2,2,2,256,512]{4,2,1,0,3:T(2,128)}), f32[2,2,2,256,512]{4,2,1,0,3:T(2,128)}, u32[]{:S(2)}, u32[]{:S(2)}) %all-to-all-start.6) | async-done | bytes 4194336 | tf_op jit(solution)/shard_map/all_to_all | solution.py:128
  403.9 7.3 %all-to-all-start.3 = ((f32[1,8,32,512]{3,2,0,1:T(8,128)}), f32[1,8,32,512]{3,2,0,1:T(8,128)S(1)}, u32[]{:S(2)}, u32[]{:S(2)}) async-start(f32[1,8,32,512]{3,2,0,1:T(8,128)} %copy.213), calls=%async_computation.3 | async-start | bytes 1048576 | tf_op jit(solution)/shard_map/all_to_all | solution.py:135
  442.4 11.9 %all-to-all-done.7 = f32[2,8,32,512]{3,2,0,1:T(8,128)S(1)} async-done(((f32[2,8,32,512]{3,2,0,1:T(8,128)}), f32[2,8,32,512]{3,2,0,1:T(8,128)S(1)}, u32[]{:S(2)}, u32[]{:S(2)}) %all-to-all-start.7) | async-done | bytes 1048608 | tf_op jit(solution)/shard_map/all_to_all | solution.py:135
  457.5 22.6 %all-reduce = (f32[512,7]{0,1:T(8,128)S(1)}, f32[512]{0:T(512)S(1)}) all-reduce(f32[512,7]{0,1:T(8,128)S(1)} %stack.87, f32[512]{0:T(512)S(1)} %get-tuple-element.39), channel_id=1, replica_groups=mesh['ctx'=8,'chan'=4] {'ctx'}, use_global_device_ids=true, to_apply=%region_7.8 | all-reduce | flops 4096 | bytes 32768 | tf_op jit(solution)/shard_map/psum | solution.py:204
  (136 shorter events, 191.6 us)
Async XLA Ops:
  7.2 50.5 %all-gather.2.cloned.1.call-start = ((), (), s32[]{:S(2)}) async-start(), calls=%async_computation.8 | async-start | bytes 2621440 | tf_op jit(solution)/shard_map/all_gather | solution.py:171
  9.1 56.6 %copy-start.4 = (f32[512,256]{0,1:T(8,128)}, f32[512,256]{0,1:T(8,128)S(1)}, u32[]{:S(2)}) copy-start(f32[512,256]{0,1:T(8,128)S(1)} %copy.185) | copy-start | bytes 1572868
  9.2 6.8 %collective-permute-start = (f32[512,6]{0,1:T(8,128)S(1)}, f32[512,6]{0,1:T(8,128)S(1)}, u32[]{:S(2)}, u32[]{:S(2)}) collective-permute-start(f32[512,6]{0,1:T(8,128)S(1)} %slice.161), channel_id=1, source_target_pairs={{0,4},{4,8},{8,12},{12,16},{16,20},{20,24},{24,28},{1,5},{5,9},{9,... | collective-permute-start | bytes 36872 | tf_op jit(solution)/shard_map/ppermute | solution.py:13
  57.6 12.4 %copy-start.16 = (f32[512,256]{1,0:T(8,128)S(1)}, f32[512,256]{1,0:T(8,128)}, u32[]{:S(2)}) copy-start(f32[512,256]{1,0:T(8,128)} %param.9) | copy-start | bytes 1572868
  65.7 4.7 copy-start.6
  65.7 11.0 %all-to-all-start.4 = ((f32[1,8,32,512]{3,2,0,1:T(8,128)}), f32[1,8,32,512]{3,2,0,1:T(8,128)S(1)}, u32[]{:S(2)}, u32[]{:S(2)}) async-start(f32[1,8,32,512]{3,2,0,1:T(8,128)} %bitcast.75), calls=%async_computation.4 | async-start | bytes 1048576 | tf_op jit(solution)/shard_map/all_to_all | solution.py:107
  76.7 18.4 %all-to-all-start = ((f32[2,8,32,512]{3,2,0,1:T(8,128)}), f32[2,8,32,512]{3,2,0,1:T(8,128)S(1)}, u32[]{:S(2)}, u32[]{:S(2)}) async-start(f32[2,8,32,512]{3,2,0,1:T(8,128)} %copy.188), calls=%async_computation | async-start | bytes 2097152 | tf_op jit(solution)/shard_map/all_to_all | solution.py:107
  95.1 30.4 %all-to-all-start.5 = ((f32[2,1,16,32,512]{4,3,1,0,2:T(8,128)}), f32[2,1,16,32,512]{4,3,1,0,2:T(8,128)S(1)}, u32[]{:S(2)}, u32[]{:S(2)}) async-start(f32[2,1,16,32,512]{4,3,1,0,2:T(8,128)} %copy.217), calls=%async_computation.5 | async-start | bytes 4194304 | tf_op jit(solution)/shard_map/all_to_all | solution.py:113
  125.5 53.9 %all-to-all-start.1 = ((f32[2,2,16,32,512]{4,3,1,0,2:T(8,128)}), f32[2,2,16,32,512]{4,3,1,0,2:T(8,128)}, u32[]{:S(2)}, u32[]{:S(2)}) async-start(f32[2,2,16,32,512]{4,3,1,0,2:T(8,128)} %copy.191), calls=%async_computation.1 | async-start | bytes 8388608 | tf_op jit(solution)/shard_map/all_to_all | solution.py:113
  136.2 7.6 %copy-start.15 = (f32[512,2,2,128]{3,2,1,0:T(2,128)}, f32[512,2,2,128]{3,2,1,0:T(2,128)S(1)}, u32[]{:S(2)}) copy-start(f32[512,2,2,128]{3,2,1,0:T(2,128)S(1)} %copy.263) | copy-start | bytes 3145732
  208.5 9.6 %copy-start.12 = (f32[2,2,512,2,128]{4,0,3,2,1:T(2,128)S(1)}, f32[2,2,512,2,128]{4,0,3,2,1:T(2,128)}, u32[]{:S(2)}) copy-start(f32[2,2,512,2,128]{4,0,3,2,1:T(2,128)} %fusion.223) | copy-start | bytes 6291460
  234.3 2.1 copy-start.8
  238.2 53.9 %copy-start.1 = (f32[1,512,2,2,128]{4,1,3,2,0:T(8,128)}, f32[1,512,2,2,128]{4,1,3,2,0:T(8,128)S(1)}, u32[]{:S(2)}) copy-start(f32[1,512,2,2,128]{4,1,3,2,0:T(8,128)S(1)} %get-tuple-element.46) | copy-start | bytes 3145732
  243.6 17.7 %copy-start.14 = (f32[512,2,2,128]{3,0,2,1:T(8,128)}, f32[512,2,2,128]{3,0,2,1:T(8,128)S(1)}, u32[]{:S(2)}) copy-start(f32[512,2,2,128]{3,0,2,1:T(8,128)S(1)} %get-tuple-element.65) | copy-start | bytes 3145732
  284.3 69.4 %all-to-all-start.2 = ((f32[2,1,2,256,512]{4,2,0,1,3:T(2,128)}), f32[2,1,2,256,512]{4,2,0,1,3:T(2,128)}, u32[]{:S(2)}, u32[]{:S(2)}) async-start(f32[2,1,2,256,512]{4,2,0,1,3:T(2,128)} %maximum_bitcast_fusion.1), calls=%async_computation.2 | async-start | bytes 4194304 | tf_op jit(solution)/shard_map/all_to_all | solution.py:128
  292.2 3.9 copy-start.2
  299.7 8.1 %copy-start.10 = (f32[2,512,2,2,128]{4,1,3,2,0:T(8,128)}, f32[2,512,2,2,128]{4,1,3,2,0:T(8,128)S(1)}, u32[]{:S(2)}) copy-start(f32[2,512,2,2,128]{4,1,3,2,0:T(8,128)S(1)} %get-tuple-element.49) | copy-start | bytes 6291460
  323.7 8.1 %copy-start.11 = (f32[2,512,2,2,128]{4,1,3,2,0:T(8,128)S(1)}, f32[2,512,2,2,128]{4,1,3,2,0:T(8,128)}, u32[]{:S(2)}) copy-start(f32[2,512,2,2,128]{4,1,3,2,0:T(8,128)} %copy-done.10) | copy-start | bytes 6291460
  341.7 6.3 %copy-start.3 = (f32[2,512,2,2,128]{1,2,0,4,3:T(2,128)S(1)}, f32[2,512,2,2,128]{1,2,0,4,3:T(2,128)}, u32[]{:S(2)}) copy-start(f32[2,512,2,2,128]{1,2,0,4,3:T(2,128)} %copy.264) | copy-start | bytes 6291460
  353.6 50.2 %all-to-all-start.6 = ((f32[2,2,2,256,512]{4,2,1,0,3:T(2,128)}), f32[2,2,2,256,512]{4,2,1,0,3:T(2,128)}, u32[]{:S(2)}, u32[]{:S(2)}) async-start(f32[2,2,2,256,512]{4,2,1,0,3:T(2,128)} %maximum_bitcast_fusion), calls=%async_computation.6 | async-start | bytes 8388608 | tf_op jit(solution)/shard_map/all_to_all | solution.py:128
  403.9 34.3 %all-to-all-start.3 = ((f32[1,8,32,512]{3,2,0,1:T(8,128)}), f32[1,8,32,512]{3,2,0,1:T(8,128)S(1)}, u32[]{:S(2)}, u32[]{:S(2)}) async-start(f32[1,8,32,512]{3,2,0,1:T(8,128)} %copy.213), calls=%async_computation.3 | async-start | bytes 1048576 | tf_op jit(solution)/shard_map/all_to_all | solution.py:135
  431.6 3.3 copy-start
  438.1 16.2 %all-to-all-start.7 = ((f32[2,8,32,512]{3,2,0,1:T(8,128)}), f32[2,8,32,512]{3,2,0,1:T(8,128)S(1)}, u32[]{:S(2)}, u32[]{:S(2)}) async-start(f32[2,8,32,512]{3,2,0,1:T(8,128)} %copy.235), calls=%async_computation.7 | async-start | bytes 2097152 | tf_op jit(solution)/shard_map/all_to_all | solution.py:135
  480.7 7.7 %collective-permute-start.1 = (f32[512,6]{0,1:T(8,128)S(1)}, f32[512,6]{0,1:T(8,128)S(1)}, u32[]{:S(2)}, u32[]{:S(2)}) collective-permute-start(f32[512,6]{0,1:T(8,128)S(1)} %slice.185), channel_id=1, source_target_pairs={{4,0},{8,4},{12,8},{16,12},{20,16},{24,20},{28,24},{5,1},{9,5},{13... | collective-permute-start | bytes 36872 | tf_op jit(solution)/shard_map/ppermute | solution.py:13
  (5 other events, 7.0 us)
Sparse Core Ops, SparseCore 0:
  9.6 48.0 all-gather.1
where the time goes:
time: 506 us; the launch traced here: 497 us
  matrix products  174 us (34%)
  waiting for transfers between devices  136 us (27%)
  local copies, waits for them, and re-layouts  74.8 us (15%)
  starting transfers between devices  60.1 us (12%)
  blocking collectives  22.6 us (4%)
  between operations  15.2 us (3%)
  other arithmetic  14.5 us (3%)
    dot_general x16, matrix products, product_with(): return jnp.einsum('...ac,ab->...bc', operand, table, precision=HIGH)  114 us
    all_gather x1, waiting for transfers between devices, per_device(): lax.all_gather(cotangent, 'chan', axis=0, tiled=True)  41.6 us
    all_to_all x2, waiting for transfers between devices, signals(): lax.all_to_all(stacked, 'ctx', split_axis=3, concat_axis=2, tiled=True)  38.7 us
    dot_general x16, matrix products, product_with(): return jnp.einsum('...a,ab->...b', operand, table, precision=HIGH)  35.5 us
    all_to_all x2, waiting for transfers between devices, spectra(): lax.all_to_all(jnp.stack((real_part, imag_part)), 'ctx', split_axis=2, co...  32.1 us
    psum x1, blocking collectives, per_device(): skip_sum, kernel_sum = lax.psum((skip_part, kernel_part), 'ctx')  22.6 us
    another operation x4, local copies, waits for them, and re-layouts, signals(): stacked = jnp.moveaxis(jnp.stack((real_part, imag_part)), 2, 4)  18.9 us
    all_to_all x2, starting transfers between devices, spectra(): lax.all_to_all(jnp.stack((real_part, imag_part)), 'ctx', split_axis=2, co...  15.6 us
  transfers between devices with their start and end apart: 11, of which 7 were waited for; matrix products, arithmetic and copies ran while one was open for 29% of the time, Pallas kernels for 0%

commit v1 on v0

--- a/solution.py
+++ b/solution.py
@@ -1,10 +1,34 @@
+import functools
 import math
 import jax
 import jax.numpy as jnp
 from jax import lax
 from jax.sharding import PartitionSpec as P
+from jax.lax import axis_index, ppermute, psum
 
 HIGH = lax.Precision.HIGHEST
+
+
+def convert_tails(u, on_dim):
+    parts_n = psum(1, "chan")
+    heard = range(parts_n)
+    kept_arr = map(lambda hop_no: (hop_no, (hop_no + 1) % parts_n), heard)
+    pages = list(kept_arr)
+    answer = range(parts_n)
+    t_next = map(lambda hop_no: (hop_no, (hop_no - 1) % parts_n), answer)
+    heap = list(t_next)
+    side_arr, prior = ([u], [u])
+    for _ in range(parts_n // 2):
+        after = ppermute(side_arr[-1], "chan", pages)
+        side_arr.append(after)
+    for _ in range((parts_n - 1) // 2):
+        high = ppermute(prior[-1], "chan", heap)
+        prior.append(high)
+    current_value = jnp.concatenate([*side_arr[::-1], *prior[1:]], on_dim)
+    return jnp.roll(current_value, (axis_index("chan") - parts_n // 2) * u.shape[on_dim], on_dim)
+
+
+time_packet = functools.partial(convert_tails, on_dim=0)
 
 
 def passed_along(block, axis, distance):
@@ -167,10 +191,7 @@
     conv_real, conv_imag = spec_product(filter_spec, value_spec, False)
     long_conv = signals(conv_real[None], conv_imag[None])[0]
     grad_mix = jnp.dot(
-        out_weight.T,
-        lax.all_gather(cotangent, "chan", axis=0, tiled=True),
-        precision=HIGH,
-        preferred_element_type=jnp.float32,
+        out_weight.T, time_packet(cotangent), precision=HIGH, preferred_element_type=jnp.float32
     )
     grad_resp = grad_mix * gate_in
     grad_real, grad_imag = spectra(grad_resp[None])

time: 506 us -> 483 us (0.955)
  waiting for transfers between devices: 136 us -> 121 us
  between operations: 15.2 us -> 1.71 us
  starting transfers between devices: 60.1 us -> 67.2 us
    all_gather x1 -> x0, waiting for transfers between devices: 41.6 us -> none  [per_device(): lax.all_gather(cotangent, 'chan', axis=0, tiled=True)]
    ppermute x0 -> x3, waiting for transfers between devices: none -> 26.8 us  [the longest x2 17.3 us: convert_tails(): after = ppermute(side_arr[-1], 'chan', pages)]
    ppermute x0 -> x3, starting transfers between devices: none -> 5.44 us  [the longest x1 3.26 us: convert_tails(): high = ppermute(prior[-1], 'chan', heap)]
  transfers between devices with their start and end apart: 11 -> 13, of which waited for: 7 -> 9; matrix products, arithmetic and copies ran while one was open for 29% -> 30% of each run, Pallas kernels for 0% -> 0%
where the time goes in v1:
time: 483 us; the launch traced here: 474 us
  matrix products  171 us (35%)
  waiting for transfers between devices  121 us (25%)
  local copies, waits for them, and re-layouts  75.8 us (16%)
  starting transfers between devices  67.2 us (14%)
  blocking collectives  22.6 us (5%)
  other arithmetic  14.6 us (3%)
    dot_general x16, matrix products, product_with(): return jnp.einsum('...ac,ab->...bc', operand, table, precision=HIGH)  115 us
    all_to_all x2, waiting for transfers between devices, signals(): lax.all_to_all(stacked, 'ctx', split_axis=3, concat_axis=2, tiled=True)  38.7 us
    dot_general x16, matrix products, product_with(): return jnp.einsum('...a,ab->...b', operand, table, precision=HIGH)  35.6 us
    all_to_all x2, waiting for transfers between devices, spectra(): lax.all_to_all(jnp.stack((real_part, imag_part)), 'ctx', split_axis=2, co...  32.4 us
    psum x1, blocking collectives, per_device(): skip_sum, kernel_sum = lax.psum((skip_part, kernel_part), 'ctx')  22.6 us
    another operation x4, local copies, waits for them, and re-layouts, signals(): stacked = jnp.moveaxis(jnp.stack((real_part, imag_part)), 2, 4)  18.7 us
    ppermute x2, waiting for transfers between devices, convert_tails(): after = ppermute(side_arr[-1], 'chan', pages)  17.3 us
    all_to_all x2, starting transfers between devices, spectra(): lax.all_to_all(jnp.stack((real_part, imag_part)), 'ctx', split_axis=2, co...  15.8 us
  transfers between devices with their start and end apart: 13, of which 9 were waited for; matrix products, arithmetic and copies ran while one was open for 30% of the time, Pallas kernels for 0%

profile of v1, /device:TPU:1, one launch (start us, length us, event | category | flops | bytes accessed | tf_op | source)
XLA Modules:
  0.0 473.9 jit_solution(3074593121745470743)
XLA Ops:
  2.8 13.9 %collective-permute-done = f32[512,256]{1,0:T(8,128)S(1)} collective-permute-done((f32[512,256]{1,0:T(8,128)}, f32[512,256]{1,0:T(8,128)S(1)}, u32[]{:S(2)}, u32[]{:S(2)}) %collective-permute-start) | collective-permute-done | bytes 524320 | tf_op jit(solution)/shard_map/ppermute | solution.py:22
  30.9 9.4 %collective-permute-done.2 = f32[512,256]{1,0:T(8,128)S(1)} collective-permute-done((f32[512,256]{1,0:T(8,128)}, f32[512,256]{1,0:T(8,128)S(1)}, u32[]{:S(2)}, u32[]{:S(2)}) %collective-permute-start.2) | collective-permute-done | bytes 524320 | tf_op jit(solution)/shard_map/ppermute | solution.py:25
  59.9 6.5 %all-to-all-start = ((f32[2,8,32,512]{3,2,0,1:T(8,128)}), f32[2,8,32,512]{3,2,0,1:T(8,128)S(1)}, u32[]{:S(2)}, u32[]{:S(2)}) async-start(f32[2,8,32,512]{3,2,0,1:T(8,128)} %copy.188), calls=%async_computation | async-start | bytes 2097152 | tf_op jit(solution)/shard_map/all_to_all | solution.py:131
  78.3 7.6 %all-to-all-start.5 = ((f32[2,1,16,32,512]{4,3,1,0,2:T(8,128)}), f32[2,1,16,32,512]{4,3,1,0,2:T(8,128)S(1)}, u32[]{:S(2)}, u32[]{:S(2)}) async-start(f32[2,1,16,32,512]{4,3,1,0,2:T(8,128)} %copy.217), calls=%async_computation.5 | async-start | bytes 4194304 | tf_op jit(solution)/shard_map/all_to_all | solution.py:137
  96.5 12.5 %all-to-all-done.5 = f32[2,1,16,32,512]{4,3,1,0,2:T(8,128)S(1)} async-done(((f32[2,1,16,32,512]{4,3,1,0,2:T(8,128)}), f32[2,1,16,32,512]{4,3,1,0,2:T(8,128)S(1)}, u32[]{:S(2)}, u32[]{:S(2)}) %all-to-all-start.5) | async-done | bytes 2097184 | tf_op jit(solution)/shard_map/all_to_all | solution.py:137
  109.0 8.2 %all-to-all-start.1 = ((f32[2,2,16,32,512]{4,3,1,0,2:T(8,128)}), f32[2,2,16,32,512]{4,3,1,0,2:T(8,128)}, u32[]{:S(2)}, u32[]{:S(2)}) async-start(f32[2,2,16,32,512]{4,3,1,0,2:T(8,128)} %copy.191), calls=%async_computation.1 | async-start | bytes 8388608 | tf_op jit(solution)/shard_map/all_to_all | solution.py:137
  142.9 19.9 %all-to-all-done.1 = f32[2,2,16,32,512]{4,3,1,0,2:T(8,128)} async-done(((f32[2,2,16,32,512]{4,3,1,0,2:T(8,128)}), f32[2,2,16,32,512]{4,3,1,0,2:T(8,128)}, u32[]{:S(2)}, u32[]{:S(2)}) %all-to-all-start.1) | async-done | bytes 4194336 | tf_op jit(solution)/shard_map/all_to_all | solution.py:137
  171.3 8.9 %fusion.226 = f32[2,2,512,2,128]{4,0,3,2,1:T(2,128)} fusion(f32[2,512,2,2,128]{4,3,2,1,0:T(2,128)S(1)} %copy.258), kind=kOutput, calls=%fused_computation.296 | convolution fusion | flops 12582968 | bytes 4194304 | tf_op jit(solution)/shard_map/...ac,ab->...bc/dot_general | solution.py:77
  180.2 8.7 %fusion.228 = f32[2,2,512,2,128]{4,0,3,2,1:T(2,128)} fusion(f32[2,512,2,2,128]{4,3,2,1,0:T(2,128)S(1)} %copy.258), kind=kOutput, calls=%fused_computation.298 | convolution fusion | flops 12582972 | bytes 4194304 | tf_op jit(solution)/shard_map/...ac,ab->...bc/dot_general | solution.py:77
  192.0 9.8 %convolution_subtract_fusion = f32[2,2,512,2,128]{4,0,3,2,1:T(2,128)S(1)} fusion(f32[2,2,512,2,128]{4,0,3,2,1:T(2,128)} %fusion.226, f32[2,512,2,2,128]{4,3,2,1,0:T(2,128)S(1)} %copy.259), kind=kOutput, calls=%fused_computation.45 | convolution fusion | flops 13107260 | bytes 6291456 | tf_op jit(solution)/shard_map/...ac,ab->...bc/dot_general | solution.py:77
  201.9 9.6 %subtract_bitcast_fusion.1 = (f32[2,512,2,2,128]{4,3,2,1,0:T(2,128)S(1)}, f32[2,512,2,2,128]{4,3,2,1,0:T(2,128)S(1)}) fusion(f32[2,2,512,2,128]{4,0,3,2,1:T(2,128)S(1)} %convolution_subtract_fusion, f32[2,128]{1,0:T(2,128)S(1)} %get-tuple-element.83, f32[2,128]{1,0:T(2,128)S(1)} %get-tuple-element.84, f32[2,2,512,2,128]{4,0,3,2,1:T(2,128)S(1)} %copy-done.13, ...), kind=kOutput, calls=%fused_computation.27 | convolution fusion | flops 16252984 | bytes 10487808 | tf_op jit(solution)/shard_map/...ac,ab->...bc/dot_general | solution.py:77
  232.1 6.1 %fusion.84 = f32[2,512,2,128]{3,0,2,1:T(2,128)} fusion(f32[512,2,2,128]{3,0,2,1:T(8,128)S(1)} %get-tuple-element.66), kind=kOutput, calls=%fused_computation.130 | convolution fusion | flops 6291512 | bytes 2097152 | tf_op jit(solution)/shard_map/...ac,ab->...bc/dot_general | solution.py:77
  253.5 7.0 %fusion.51 = f32[1,512,2,2,128]{4,3,2,1,0:T(2,128)} fusion(f32[2,512,2,128]{3,0,2,1:T(2,128)} %fusion.84, f32[512,2,2,128]{3,0,2,1:T(8,128)} %copy-done.16), kind=kOutput, calls=%fused_computation.80 | convolution fusion | flops 6553656 | bytes 3145728 | tf_op jit(solution)/shard_map/...ac,ab->...bc/dot_general | solution.py:77
  267.9 7.9 %all-to-all-start.2 = ((f32[2,1,2,256,512]{4,2,0,1,3:T(2,128)}), f32[2,1,2,256,512]{4,2,0,1,3:T(2,128)}, u32[]{:S(2)}, u32[]{:S(2)}) async-start(f32[2,1,2,256,512]{4,2,0,1,3:T(2,128)} %maximum_bitcast_fusion.1), calls=%async_computation.2 | async-start | bytes 4194304 | tf_op jit(solution)/shard_map/all_to_all | solution.py:152
  283.3 8.1 %fusion.38 = f32[2,2,512,2,128]{4,0,3,2,1:T(2,128)S(1)} fusion(f32[2,512,2,2,128]{4,1,3,2,0:T(8,128)S(1)} %get-tuple-element.50), kind=kOutput, calls=%fused_computation.52 | convolution fusion | flops 12582968 | bytes 4194304 | tf_op jit(solution)/shard_map/...ac,ab->...bc/dot_general | solution.py:77
  291.4 9.9 %subtract_bitcast_fusion = f32[2,512,2,2,128]{4,3,2,1,0:T(2,128)} fusion(f32[2,2,512,2,128]{4,0,3,2,1:T(2,128)S(1)} %fusion.38, f32[2,512,2,2,128]{4,1,3,2,0:T(8,128)S(1)} %get-tuple-element.49), kind=kOutput, calls=%fused_computation.23 | convolution fusion | flops 13107256 | bytes 6291456 | tf_op jit(solution)/shard_map/...ac,ab->...bc/dot_general | solution.py:77
  301.3 6.1 %copy.264 = f32[2,512,2,2,128]{1,2,0,4,3:T(2,128)} copy(f32[2,512,2,2,128]{4,3,2,1,0:T(2,128)} %subtract_bitcast_fusion) | data formatting | bytes 4194304 | tf_op jit(solution)/shard_map/stack;reshape | solution.py:151
  307.4 8.0 %fusion.36 = f32[2,2,512,2,128]{4,0,3,2,1:T(2,128)S(1)} fusion(f32[2,512,2,2,128]{4,1,3,2,0:T(8,128)S(1)} %get-tuple-element.50), kind=kOutput, calls=%fused_computation.50 | convolution fusion | flops 12582968 | bytes 4194304 | tf_op jit(solution)/shard_map/...ac,ab->...bc/dot_general | solution.py:77
  315.4 10.1 %add_bitcast_fusion = f32[2,512,2,2,128]{4,3,2,1,0:T(2,128)} fusion(f32[2,2,512,2,128]{4,0,3,2,1:T(2,128)S(1)} %fusion.36, f32[2,512,2,2,128]{4,1,3,2,0:T(8,128)S(1)} %copy-done.12), kind=kOutput, calls=%fused_computation.22 | convolution fusion | flops 13107256 | bytes 6291456 | tf_op jit(solution)/shard_map/...ac,ab->...bc/dot_general | solution.py:77
  325.5 6.3 %copy.265 = f32[2,512,2,2,128]{1,2,0,4,3:T(2,128)} copy(f32[2,512,2,2,128]{4,3,2,1,0:T(2,128)} %add_bitcast_fusion) | data formatting | bytes 4194304 | tf_op jit(solution)/shard_map/stack;reshape | solution.py:151
  349.0 38.7 %all-to-all-done.6 = f32[2,2,2,256,512]{4,2,1,0,3:T(2,128)} async-done(((f32[2,2,2,256,512]{4,2,1,0,3:T(2,128)}), f32[2,2,2,256,512]{4,2,1,0,3:T(2,128)}, u32[]{:S(2)}, u32[]{:S(2)}) %all-to-all-start.6) | async-done | bytes 4194336 | tf_op jit(solution)/shard_map/all_to_all | solution.py:152
  387.7 7.2 %all-to-all-start.3 = ((f32[1,8,32,512]{3,2,0,1:T(8,128)}), f32[1,8,32,512]{3,2,0,1:T(8,128)S(1)}, u32[]{:S(2)}, u32[]{:S(2)}) async-start(f32[1,8,32,512]{3,2,0,1:T(8,128)} %copy.213), calls=%async_computation.3 | async-start | bytes 1048576 | tf_op jit(solution)/shard_map/all_to_all | solution.py:159
  426.2 11.9 %all-to-all-done.7 = f32[2,8,32,512]{3,2,0,1:T(8,128)S(1)} async-done(((f32[2,8,32,512]{3,2,0,1:T(8,128)}), f32[2,8,32,512]{3,2,0,1:T(8,128)S(1)}, u32[]{:S(2)}, u32[]{:S(2)}) %all-to-all-start.7) | async-done | bytes 1048608 | tf_op jit(solution)/shard_map/all_to_all | solution.py:159
  441.3 22.6 %all-reduce = (f32[512,7]{0,1:T(8,128)S(1)}, f32[512]{0:T(512)S(1)}) all-reduce(f32[512,7]{0,1:T(8,128)S(1)} %stack.87, f32[512]{0:T(512)S(1)} %get-tuple-element.39), channel_id=1, replica_groups=mesh['ctx'=8,'chan'=4] {'ctx'}, use_global_device_ids=true, to_apply=%region_7.8 | all-reduce | flops 4096 | bytes 32768 | tf_op jit(solution)/shard_map/psum | solution.py:225
  (153 shorter events, 207.2 us)
Async XLA Ops:
  0.6 30.2 %copy-start.14 = (f32[512,256]{1,0:T(8,128)S(1)}, f32[512,256]{1,0:T(8,128)}, u32[]{:S(2)}) copy-start(f32[512,256]{1,0:T(8,128)} %param.13) | copy-start | bytes 1572868
  0.6 26.7 %copy-start.19 = (f32[512,7]{0,1:T(8,128)S(1)}, f32[512,7]{0,1:T(8,128)}, u32[]{:S(2)}) copy-start(f32[512,7]{0,1:T(8,128)} %param.10) | copy-start | bytes 43012
  0.7 16.1 %collective-permute-start = (f32[512,256]{1,0:T(8,128)}, f32[512,256]{1,0:T(8,128)S(1)}, u32[]{:S(2)}, u32[]{:S(2)}) collective-permute-start(f32[512,256]{1,0:T(8,128)} %param.13), channel_id=1, source_target_pairs={{0,1},{1,2},{2,3},{3,0},{4,5},{5,6},{6,7},{7,4},{8,9},{9,10},{10,1... | collective-permute-start | bytes 1572872 | tf_op jit(solution)/shard_map/ppermute | solution.py:22
  16.7 14.1 %collective-permute-start.1 = (f32[512,256]{1,0:T(8,128)S(1)}, f32[512,256]{1,0:T(8,128)S(1)}, u32[]{:S(2)}, u32[]{:S(2)}) collective-permute-start(f32[512,256]{1,0:T(8,128)S(1)} %collective-permute-done), channel_id=1, source_target_pairs={{0,1},{1,2},{2,3},{3,0},{4,5},{5,6},{6,7},{7,4},{8,9},{9,10},{10,1... | collective-permute-start | bytes 1572872 | tf_op jit(solution)/shard_map/ppermute | solution.py:22
  16.7 23.6 %collective-permute-start.2 = (f32[512,256]{1,0:T(8,128)}, f32[512,256]{1,0:T(8,128)S(1)}, u32[]{:S(2)}, u32[]{:S(2)}) collective-permute-start(f32[512,256]{1,0:T(8,128)} %param.13), channel_id=1, source_target_pairs={{0,3},{1,0},{2,1},{3,2},{4,7},{5,4},{6,5},{7,6},{8,11},{9,8},{10,9... | collective-permute-start | bytes 1572872 | tf_op jit(solution)/shard_map/ppermute | solution.py:25
  21.2 19.4 %copy-start.4 = (f32[512,256]{0,1:T(8,128)}, f32[512,256]{0,1:T(8,128)S(1)}, u32[]{:S(2)}) copy-start(f32[512,256]{0,1:T(8,128)S(1)} %copy.185) | copy-start | bytes 1572868
  21.2 19.3 %collective-permute-start.3 = (f32[512,6]{0,1:T(8,128)S(1)}, f32[512,6]{0,1:T(8,128)S(1)}, u32[]{:S(2)}, u32[]{:S(2)}) collective-permute-start(f32[512,6]{0,1:T(8,128)S(1)} %slice.161), channel_id=1, source_target_pairs={{0,4},{4,8},{8,12},{12,16},{16,20},{20,24},{24,28},{1,5},{5,9},{9,... | collective-permute-start | bytes 36872 | tf_op jit(solution)/shard_map/ppermute | solution.py:37
  42.6 10.6 %copy-start.18 = (f32[512,256]{1,0:T(8,128)S(1)}, f32[512,256]{1,0:T(8,128)}, u32[]{:S(2)}) copy-start(f32[512,256]{1,0:T(8,128)} %param.9) | copy-start | bytes 1572868
  47.6 12.3 %all-to-all-start.4 = ((f32[1,8,32,512]{3,2,0,1:T(8,128)}), f32[1,8,32,512]{3,2,0,1:T(8,128)S(1)}, u32[]{:S(2)}, u32[]{:S(2)}) async-start(f32[1,8,32,512]{3,2,0,1:T(8,128)} %bitcast.76), calls=%async_computation.4 | async-start | bytes 1048576 | tf_op jit(solution)/shard_map/all_to_all | solution.py:131
  59.9 18.4 %all-to-all-start = ((f32[2,8,32,512]{3,2,0,1:T(8,128)}), f32[2,8,32,512]{3,2,0,1:T(8,128)S(1)}, u32[]{:S(2)}, u32[]{:S(2)}) async-start(f32[2,8,32,512]{3,2,0,1:T(8,128)} %copy.188), calls=%async_computation | async-start | bytes 2097152 | tf_op jit(solution)/shard_map/all_to_all | solution.py:131
  78.3 30.7 %all-to-all-start.5 = ((f32[2,1,16,32,512]{4,3,1,0,2:T(8,128)}), f32[2,1,16,32,512]{4,3,1,0,2:T(8,128)S(1)}, u32[]{:S(2)}, u32[]{:S(2)}) async-start(f32[2,1,16,32,512]{4,3,1,0,2:T(8,128)} %copy.217), calls=%async_computation.5 | async-start | bytes 4194304 | tf_op jit(solution)/shard_map/all_to_all | solution.py:137
  109.0 53.8 %all-to-all-start.1 = ((f32[2,2,16,32,512]{4,3,1,0,2:T(8,128)}), f32[2,2,16,32,512]{4,3,1,0,2:T(8,128)}, u32[]{:S(2)}, u32[]{:S(2)}) async-start(f32[2,2,16,32,512]{4,3,1,0,2:T(8,128)} %copy.191), calls=%async_computation.1 | async-start | bytes 8388608 | tf_op jit(solution)/shard_map/all_to_all | solution.py:137
  119.6 7.6 %copy-start.17 = (f32[512,2,2,128]{3,2,1,0:T(2,128)}, f32[512,2,2,128]{3,2,1,0:T(2,128)S(1)}, u32[]{:S(2)}) copy-start(f32[512,2,2,128]{3,2,1,0:T(2,128)S(1)} %copy.263) | copy-start | bytes 3145732
  192.0 9.9 %copy-start.13 = (f32[2,2,512,2,128]{4,0,3,2,1:T(2,128)S(1)}, f32[2,2,512,2,128]{4,0,3,2,1:T(2,128)}, u32[]{:S(2)}) copy-start(f32[2,2,512,2,128]{4,0,3,2,1:T(2,128)} %fusion.228) | copy-start | bytes 6291460
  221.8 53.9 %copy-start.1 = (f32[1,512,2,2,128]{4,1,3,2,0:T(8,128)}, f32[1,512,2,2,128]{4,1,3,2,0:T(8,128)S(1)}, u32[]{:S(2)}) copy-start(f32[1,512,2,2,128]{4,1,3,2,0:T(8,128)S(1)} %get-tuple-element.46) | copy-start | bytes 3145732
  227.2 17.9 %copy-start.16 = (f32[512,2,2,128]{3,0,2,1:T(8,128)}, f32[512,2,2,128]{3,0,2,1:T(8,128)S(1)}, u32[]{:S(2)}) copy-start(f32[512,2,2,128]{3,0,2,1:T(8,128)S(1)} %get-tuple-element.65) | copy-start | bytes 3145732
  267.9 69.6 %all-to-all-start.2 = ((f32[2,1,2,256,512]{4,2,0,1,3:T(2,128)}), f32[2,1,2,256,512]{4,2,0,1,3:T(2,128)}, u32[]{:S(2)}, u32[]{:S(2)}) async-start(f32[2,1,2,256,512]{4,2,0,1,3:T(2,128)} %maximum_bitcast_fusion.1), calls=%async_computation.2 | async-start | bytes 4194304 | tf_op jit(solution)/shard_map/all_to_all | solution.py:152
  283.3 8.1 %copy-start.11 = (f32[2,512,2,2,128]{4,1,3,2,0:T(8,128)}, f32[2,512,2,2,128]{4,1,3,2,0:T(8,128)S(1)}, u32[]{:S(2)}) copy-start(f32[2,512,2,2,128]{4,1,3,2,0:T(8,128)S(1)} %get-tuple-element.49) | copy-start | bytes 6291460
  307.4 8.1 %copy-start.12 = (f32[2,512,2,2,128]{4,1,3,2,0:T(8,128)S(1)}, f32[2,512,2,2,128]{4,1,3,2,0:T(8,128)}, u32[]{:S(2)}) copy-start(f32[2,512,2,2,128]{4,1,3,2,0:T(8,128)} %copy-done.11) | copy-start | bytes 6291460
  325.5 6.3 %copy-start.3 = (f32[2,512,2,2,128]{1,2,0,4,3:T(2,128)S(1)}, f32[2,512,2,2,128]{1,2,0,4,3:T(2,128)}, u32[]{:S(2)}) copy-start(f32[2,512,2,2,128]{1,2,0,4,3:T(2,128)} %copy.264) | copy-start | bytes 6291460
  337.5 50.2 %all-to-all-start.6 = ((f32[2,2,2,256,512]{4,2,1,0,3:T(2,128)}), f32[2,2,2,256,512]{4,2,1,0,3:T(2,128)}, u32[]{:S(2)}, u32[]{:S(2)}) async-start(f32[2,2,2,256,512]{4,2,1,0,3:T(2,128)} %maximum_bitcast_fusion), calls=%async_computation.6 | async-start | bytes 8388608 | tf_op jit(solution)/shard_map/all_to_all | solution.py:152
  387.7 34.2 %all-to-all-start.3 = ((f32[1,8,32,512]{3,2,0,1:T(8,128)}), f32[1,8,32,512]{3,2,0,1:T(8,128)S(1)}, u32[]{:S(2)}, u32[]{:S(2)}) async-start(f32[1,8,32,512]{3,2,0,1:T(8,128)} %copy.213), calls=%async_computation.3 | async-start | bytes 1048576 | tf_op jit(solution)/shard_map/all_to_all | solution.py:159
  421.9 16.2 %all-to-all-start.7 = ((f32[2,8,32,512]{3,2,0,1:T(8,128)}), f32[2,8,32,512]{3,2,0,1:T(8,128)S(1)}, u32[]{:S(2)}, u32[]{:S(2)}) async-start(f32[2,8,32,512]{3,2,0,1:T(8,128)} %copy.235), calls=%async_computation.7 | async-start | bytes 2097152 | tf_op jit(solution)/shard_map/all_to_all | solution.py:159
  464.5 7.7 %collective-permute-start.4 = (f32[512,6]{0,1:T(8,128)S(1)}, f32[512,6]{0,1:T(8,128)S(1)}, u32[]{:S(2)}, u32[]{:S(2)}) collective-permute-start(f32[512,6]{0,1:T(8,128)S(1)} %slice.185), channel_id=1, source_target_pairs={{4,0},{8,4},{12,8},{16,12},{20,16},{24,20},{28,24},{5,1},{9,5},{13... | collective-permute-start | bytes 36872 | tf_op jit(solution)/shard_map/ppermute | solution.py:37
  (10 other events, 24.4 us)
